TPU v7x, 128 devices: a whole 4x4x4 slice. The times are simulated.
128 devices in a mesh: seq: 32 (over x, y, core), tp: 4 (over z).
Axes of the slice: x: 4, y: 4, z: 4, core: 2. Of those that a mesh axis runs over, the one named last changes fastest.
Arguments:
- token_ids: int32 [64, 4], replicated, may hold values from 0 to 51199
- embedding: bfloat16 [51200, 2048], P(('seq', 'tp')), may hold values from -8 to 8
- group_of: int32 [64], replicated, may hold values from 0 to 7, as said below
- prefix_len: int32 [8], replicated, may hold values from 1 to 2048, as said below
- tail_len: int32 [64], replicated, may hold values from 1 to 512, as said below
- block_map: int32 [512, 2], P('seq'), may hold values from -1 to 71, as said below
- k_cache: bfloat16 [2, 65536, 2048], P(None, 'seq', 'tp'), may hold values from -100 to 100
- v_cache: bfloat16 [2, 65536, 2048], P(None, 'seq', 'tp'), may hold values from -12 to 12
- ln_gain: float32 [2, 2048], replicated, may hold values from 0.25 to 1.75
- ln_bias: float32 [2, 2048], replicated, may hold values from -1.5 to 1.5
- w_qkv: bfloat16 [2, 2048, 3, 2048], P(None, 'seq', None, 'tp'), may hold values from -0.125 to 0.125
- w_fc1: bfloat16 [2, 2048, 8192], P(None, 'seq', 'tp'), may hold values from -0.125 to 0.125
- b_fc1: float32 [2, 8192], P(None, 'tp'), may hold values from -2.5 to 2.5
- w_out: bfloat16 [2, 2048, 2048], P(None, ('tp', 'seq')), may hold values from -0.125 to 0.125
- w_fc2: bfloat16 [2, 8192, 2048], P(None, ('tp', 'seq')), may hold values from -0.0625 to 0.0625
Outputs:
- hidden_out: float32 [64, 4, 2048], replicated
Inputs may be any that keep to these rules, and one draw needn't show every extreme that they name: `group_of`: every group holds exactly 8 requests. `prefix_len`: some group's prompt is 2048 long. `tail_len`: some request's tail is 512 long. `block_map`: row b gives the segment held by cache block b (slots b * 128 to b * 128 + 127): g for group g's prompt, 8 + r for request r's tail, -1 for none; and its rank within the segment. A segment of length L holds ranks 0 to ceil(L / 128) - 1, each in exactly one block; a block with segment -1 has rank 0.
All inputs are finite; a program needn't handle non-finite values.
Results may differ from a plain program's by a relative error of at most 0.04.
The roundings to bfloat16 on the way count: a program that leaves them out, or rounds other values in their place, can miss the bound.
Values may be sent and summed in bfloat16 or wider, within the bound.
A program may use at most 192 MiB of HBM per device.

v0:
```python
import math

import jax
import jax.numpy as jnp
from jax import lax
from jax.sharding import PartitionSpec as P

HEADS = 32
HEAD_DIM = 64
ROT = 32
LAYERS = 2
BLOCK = 128
SPAN = 512


very_negative = -1e30


def layer_norm(values, gain_row, bias_row):
    average = jnp.mean(values, axis=-1, keepdims=True)
    centred = values - average
    variance = jnp.mean(centred * centred, axis=-1, keepdims=True)
    return centred * lax.rsqrt(variance + 1e-05) * gain_row + bias_row


def rotary(values, positions):
    half_width = ROT // 2
    frequency = jnp.exp(
        jnp.arange(half_width, dtype=jnp.float32) * (-2.0 * math.log(10000.0) / ROT)
    )
    angles = positions.astype(jnp.float32)[:, None] * frequency[None, :]
    cosine = jnp.cos(angles)[:, None, :]
    sine_part = jnp.sin(angles)[:, None, :]
    low_half = values[..., :half_width]
    high_half = values[..., half_width:ROT]
    return jnp.concatenate(
        [
            low_half * cosine - high_half * sine_part,
            high_half * cosine + low_half * sine_part,
            values[..., ROT:],
        ],
        axis=-1,
    )


def combine_parts(left_part, right_part):
    max_left, sum_left, out_left = left_part
    max_right, sum_right, out_right = right_part
    top_value = jnp.maximum(max_left, max_right)
    scale_left = jnp.exp(max_left - top_value)
    scale_right = jnp.exp(max_right - top_value)
    return (
        top_value,
        sum_left * scale_left + sum_right * scale_right,
        out_left * scale_left[..., None] + out_right * scale_right[..., None],
    )


def full_total(values):
    return lax.psum(values, ("seq", "tp"))


def per_device(
    token_ids,
    embedding,
    group_of,
    prefix_len,
    tail_len,
    block_map,
    k_cache,
    v_cache,
    ln_gain,
    ln_bias,
    w_qkv,
    w_fc1,
    b_fc1,
    w_out,
    w_fc2,
):
    tp_count = lax.axis_size("tp")
    seq_index = lax.axis_index("seq")
    tp_index = lax.axis_index("tp")
    requests = token_ids.shape[0]
    new_tokens = token_ids.shape[1]
    groups = prefix_len.shape[0]
    heads_local = HEADS // tp_count
    width_local = heads_local * HEAD_DIM
    score_scale = 1.0 / math.sqrt(HEAD_DIM)
    vocab_rows = embedding.shape[0]
    first_row = (seq_index * tp_count + tp_index) * vocab_rows
    local_ids = token_ids.reshape(-1) - first_row
    inside = (local_ids >= 0) & (local_ids < vocab_rows)
    picked = jnp.take(embedding, jnp.clip(local_ids, 0, vocab_rows - 1), axis=0).astype(jnp.float32)
    picked = jnp.where(inside[:, None], picked, 0.0)
    start_states = full_total(picked).reshape(requests, new_tokens, -1)
    group_hit = group_of[:, None] == jnp.arange(groups, dtype=jnp.int32)[None, :]
    shared_len = jnp.sum(jnp.where(group_hit, prefix_len[None, :], 0), axis=1)
    base_positions = shared_len + tail_len
    seg_len = jnp.concatenate([prefix_len, tail_len])
    seg_count = seg_len.shape[0]
    blocks_local = block_map.shape[0]
    seg_blk = block_map[:, 0]
    rank_blk = block_map[:, 1]
    seg_hit = seg_blk[:, None] == jnp.arange(seg_count, dtype=jnp.int32)[None, :]
    len_blk = jnp.sum(jnp.where(seg_hit, seg_len[None, :], 0), axis=1)
    slot_positions = rank_blk[:, None] * BLOCK + jnp.arange(BLOCK, dtype=jnp.int32)[None, :]
    live_slot = ((seg_blk[:, None] >= 0) & (slot_positions < len_blk[:, None])).reshape(-1)
    seg_slot = jnp.broadcast_to(seg_blk[:, None], (blocks_local, BLOCK)).reshape(-1)
    own_tail = seg_slot[None, :] == (groups + jnp.arange(requests, dtype=jnp.int32))[:, None]
    own_prompt = seg_slot[None, :] == group_of[:, None]
    allowed = (own_tail | own_prompt) & live_slot[None, :]
    step_count = allowed.shape[1] // SPAN
    allowed_steps = allowed.reshape(requests, step_count, SPAN).transpose(1, 0, 2)
    rows_local = w_qkv.shape[1]
    unit_count = w_fc2.shape[1]
    sub_width = w_out.shape[1]
    token_index = jnp.arange(new_tokens, dtype=jnp.int32)
    new_keys = [
        jnp.zeros((requests, new_tokens, heads_local, HEAD_DIM), jnp.bfloat16)
        for layer_index in range(LAYERS)
    ]
    new_values = [
        jnp.zeros((requests, new_tokens, heads_local, HEAD_DIM), jnp.bfloat16)
        for layer_index in range(LAYERS)
    ]
    results = []
    for token_step in range(new_tokens):
        hidden_state = start_states[:, token_step]
        positions = base_positions + token_step
        for layer_index in range(LAYERS):
            normed = layer_norm(hidden_state, ln_gain[layer_index], ln_bias[layer_index]).astype(
                jnp.bfloat16
            )
            my_rows = lax.dynamic_slice_in_dim(normed, seq_index * rows_local, rows_local, 1)
            part_proj = jnp.dot(
                my_rows,
                w_qkv[layer_index].reshape(rows_local, -1),
                preferred_element_type=jnp.float32,
            )
            part_fc1 = jnp.dot(my_rows, w_fc1[layer_index], preferred_element_type=jnp.float32)
            attention_proj, fc1_all = lax.psum((part_proj, part_fc1), "seq")
            pre_act = lax.dynamic_slice_in_dim(fc1_all, seq_index * unit_count, unit_count, 1)
            pre_act = (
                pre_act
                + lax.dynamic_slice_in_dim(
                    b_fc1[layer_index], seq_index * unit_count, unit_count, 0
                )[None, :]
            )
            activated = jax.nn.gelu(pre_act, approximate=True).astype(jnp.bfloat16)
            attention_proj = attention_proj.reshape(requests, 3, heads_local, HEAD_DIM)
            queries = rotary(attention_proj[:, 0], positions).astype(jnp.bfloat16)
            key_rows = rotary(attention_proj[:, 1], positions).astype(jnp.bfloat16)
            value_rows = attention_proj[:, 2].astype(jnp.bfloat16)
            new_keys[layer_index] = new_keys[layer_index].at[:, token_step].set(key_rows)
            new_values[layer_index] = new_values[layer_index].at[:, token_step].set(value_rows)
            key_steps = k_cache[layer_index].reshape(step_count, SPAN, heads_local, HEAD_DIM)
            value_steps = v_cache[layer_index].reshape(step_count, SPAN, heads_local, HEAD_DIM)

            def cache_step(carry, inputs):
                run_max, run_sum, run_out = carry
                key_block, value_block, allow_block = inputs
                scores = (
                    jnp.einsum(
                        "rhd,shd->hrs", queries, key_block, preferred_element_type=jnp.float32
                    )
                    * score_scale
                )
                scores = jnp.where(allow_block[None], scores, very_negative)
                next_max = jnp.maximum(run_max, jnp.max(scores, axis=2))
                weights = jnp.where(allow_block[None], jnp.exp(scores - next_max[..., None]), 0.0)
                shrink = jnp.exp(run_max - next_max)
                next_sum = run_sum * shrink + jnp.sum(weights, axis=2)
                next_out = run_out * shrink[..., None] + jnp.einsum(
                    "hrs,shd->hrd",
                    weights.astype(jnp.bfloat16),
                    value_block,
                    preferred_element_type=jnp.float32,
                )
                return ((next_max, next_sum, next_out), None)

            start_carry = (
                jnp.full((heads_local, requests), very_negative, jnp.float32),
                jnp.zeros((heads_local, requests), jnp.float32),
                jnp.zeros((heads_local, requests, HEAD_DIM), jnp.float32),
            )
            (part_max, part_sum, part_out), unused = lax.scan(
                cache_step, start_carry, (key_steps, value_steps, allowed_steps)
            )
            cache_max = lax.pmax(part_max, "seq")
            factor = jnp.exp(part_max - cache_max)
            cache_sum, cache_out = (
                lax.psum((part_sum * factor).astype(jnp.bfloat16), "seq").astype(jnp.float32),
                lax.psum((part_out * factor[..., None]).astype(jnp.bfloat16), "seq").astype(
                    jnp.float32
                ),
            )
            visible = (token_index <= token_step)[None, None, :]
            fresh_scores = (
                jnp.einsum(
                    "rhd,rjhd->hrj",
                    queries,
                    new_keys[layer_index],
                    preferred_element_type=jnp.float32,
                )
                * score_scale
            )
            fresh_scores = jnp.where(visible, fresh_scores, very_negative)
            fresh_max = jnp.max(fresh_scores, axis=2)
            fresh_weights = jnp.where(visible, jnp.exp(fresh_scores - fresh_max[..., None]), 0.0)
            fresh_sum = jnp.sum(fresh_weights, axis=2)
            fresh_out = jnp.einsum(
                "hrj,rjhd->hrd",
                fresh_weights.astype(jnp.bfloat16),
                new_values[layer_index],
                preferred_element_type=jnp.float32,
            )
            joint_max, denom_total, weighted = combine_parts(
                (cache_max, cache_sum, cache_out), (fresh_max, fresh_sum, fresh_out)
            )
            attended = (weighted / denom_total[..., None]).astype(jnp.bfloat16)
            attended = attended.transpose(1, 0, 2).reshape(requests, width_local)
            my_cols = lax.dynamic_slice_in_dim(attended, seq_index * sub_width, sub_width, 1)
            update = jnp.dot(my_cols, w_out[layer_index], preferred_element_type=jnp.float32)
            update = update + jnp.dot(
                activated, w_fc2[layer_index], preferred_element_type=jnp.float32
            )
            hidden_state = hidden_state + full_total(update)
        results.append(hidden_state)
    stacked = jnp.stack(results, axis=1)
    return stacked


def solution(mesh):
    in_specs = (
        P(),
        P(("seq", "tp"), None),
        P(),
        P(),
        P(),
        P("seq", None),
        P(None, "seq", "tp"),
        P(None, "seq", "tp"),
        P(),
        P(),
        P(None, "seq", None, "tp"),
        P(None, "seq", "tp"),
        P(None, "tp"),
        P(None, ("tp", "seq"), None),
        P(None, ("tp", "seq"), None),
    )
    out_specs = P()
    return jax.shard_map(
        per_device, mesh=mesh, in_specs=in_specs, out_specs=out_specs, check_vma=False
    )
```

profile of v0, /device:TPU:25, one launch (start us, length us, event | category | flops | bytes accessed | tf_op | source)
XLA Modules:
  0.0 1579.7 jit_solution(3795356926570926883)
XLA Ops:
  28.1 140.2 %all-reduce.22.cloned.1.call-done = f32[64,4,2048]{2,0,1:T(8,128)} async-done(((f32[64,4,2048]{2,0,1:T(8,128)}), f32[64,4,2048]{2,0,1:T(8,128)}) %all-reduce.22.cloned.1.call-update) | async-done | bytes 2097168 | tf_op jit(solution)/shard_map/psum | solution.py:60
  195.0 6.2 reshape.1365
  201.2 5.6 copy.77
  208.9 91.1 %all-reduce.30.cloned.1.call-done = (f32[64,3,8,64]{3,0,2,1:T(8,128)}, f32[64,3,8,64]{3,0,2,1:T(8,128)}, f32[64,3,8,64]{3,0,2,1:T(8,128)}, f32[64,3,8,64]{3,0,2,...) async-done(((f32[64,3,8,64]{3,0,2,1:T(8,128)}, f32[64,3,8,64]{3,0,2,1:T(8,128)}, f32[64,3,8,64]{3,0,2,1:T(8,128)}, ...) | async-done | bytes 3670032 | tf_op jit(solution)/shard_map/psum | solution.py:141
  362.2 12.6 while.142
  374.8 12.8 while.140
  387.6 9.0 while.138
  396.6 9.0 while.136
  407.6 107.9 %all-reduce.9 = (f32[8,64]{1,0:T(8,128)S(1)}, f32[8,64]{1,0:T(8,128)S(1)}, f32[8,64]{1,0:T(8,128)S(1)}, f32[8,64]{1,0:T(8,128)S(1)}) all-reduce(f32[8,64]{1,0:T(8,128)S(1)} %get-tuple-element.568, f32[8,64]{1,0:T(8,128)S(1)} %get-tuple-element.550, f32[8,64]{1,0:T(8,128)S(1)} %get-tuple-element.556, ...), channel_id=1, replica_groups=mesh['seq'=32,'tp'=4] {'seq'}, use_global_device_ids=true, to_apply=%region_94.95 | all-reduce | flops 2048 | bytes 16384 | tf_op jit(solution)/shard_map/pmax | solution.py:189
  521.4 68.5 %all-reduce.11 = (bf16[8,64]{1,0:T(8,128)(2,1)S(1)}, bf16[8,64]{1,0:T(8,128)(2,1)S(1)}, bf16[8,64]{1,0:T(8,128)(2,1)S(1)}, bf16[8,64]{1,0:T(8,128)(2,1)S(1)}) all-reduce(bf16[8,64]{1,0:T(8,128)(2,1)S(1)} %get-tuple-element.1165, bf16[8,64]{1,0:T(8,128)(2,1)S(1)} %get-tuple-element.1163, ...), channel_id=1, replica_groups=mesh['seq'=32,'tp'=4] {'seq'}, use_global_device_ids=true, to_apply=%region_97.98 | all-reduce | flops 2048 | bytes 8192 | tf_op jit(solution)/shard_map/psum | solution.py:192
  590.2 114.7 %all-reduce.34.cloned.1.call-done = (bf16[8,64,64]{2,1,0:T(8,128)(2,1)}, bf16[8,64,64]{2,1,0:T(8,128)(2,1)}, bf16[8,64,64]{2,1,0:T(8,128)(2,1)}, bf16[8,64,64]{2,1,0:T(8,128)(2,1)}) async-done(((bf16[8,64,64]{2,1,0:T(8,128)(2,1)}, bf16[8,64,64]{2,1,0:T(8,128)(2,1)}, bf16[8,64,64]{2,1,0:T(8,128)(2,1)}, bf16[8,64,64]{2,1,0:T(8,128)(2,1)}), (bf16[8,64,64]{2,1,0:T(8,128)(2,1)}, bf16[8,64,64]{2,1,0:T(8,128)(2,1)}, ...) | async-done | bytes 262160 | tf_op jit(solution)/shard_map/psum | solution.py:193
  719.4 149.4 %all-reduce.26.cloned.1.call-done = (f32[64,2048]{1,0:T(8,128)}, f32[64,2048]{1,0:T(8,128)}, f32[64,2048]{1,0:T(8,128)}, f32[64,2048]{1,0:T(8,128)}) async-done(((f32[64,2048]{1,0:T(8,128)}, f32[64,2048]{1,0:T(8,128)}, f32[64,2048]{1,0:T(8,128)}, f32[64,2048]{1,0:T(8,128)}), (f32[64,2048]{1,0:T(8,128)}, f32[64,2048]{1,0:T(8,128)}, f32[64,2048]{1,0:T(8,128)}, ...) | async-done | bytes 2097168 | tf_op jit(solution)/shard_map/psum | solution.py:60
  887.9 4.5 copy.83
  892.4 6.2 reshape.1367
  898.6 5.5 copy.84
  905.4 90.4 %all-reduce.28.cloned.1.call-done = (f32[64,3,8,64]{3,0,2,1:T(8,128)}, f32[64,3,8,64]{3,0,2,1:T(8,128)}, f32[64,3,8,64]{3,0,2,1:T(8,128)}, f32[64,3,8,64]{3,0,2,...) async-done(((f32[64,3,8,64]{3,0,2,1:T(8,128)}, f32[64,3,8,64]{3,0,2,1:T(8,128)}, f32[64,3,8,64]{3,0,2,1:T(8,128)}, ...) | async-done | bytes 3670032 | tf_op jit(solution)/shard_map/psum | solution.py:141
  1010.9 12.6 while.137
  1040.5 12.6 while.139
  1068.2 9.1 while.141
  1095.3 9.0 while.143
  1104.7 107.8 %all-reduce.8 = (f32[8,64]{1,0:T(8,128)S(1)}, f32[8,64]{1,0:T(8,128)S(1)}, f32[8,64]{1,0:T(8,128)S(1)}, f32[8,64]{1,0:T(8,128)S(1)}) all-reduce(f32[8,64]{1,0:T(8,128)S(1)} %get-tuple-element.571, f32[8,64]{1,0:T(8,128)S(1)} %get-tuple-element.565, f32[8,64]{1,0:T(8,128)S(1)} %get-tuple-element.559, ...), channel_id=1, replica_groups=mesh['seq'=32,'tp'=4] {'seq'}, use_global_device_ids=true, to_apply=%region_108.109 | all-reduce | flops 2048 | bytes 16384 | tf_op jit(solution)/shard_map/pmax | solution.py:189
  1218.4 68.5 %all-reduce.10 = (bf16[8,64]{1,0:T(8,128)(2,1)S(1)}, bf16[8,64]{1,0:T(8,128)(2,1)S(1)}, bf16[8,64]{1,0:T(8,128)(2,1)S(1)}, bf16[8,64]{1,0:T(8,128)(2,1)S(1)}) all-reduce(bf16[8,64]{1,0:T(8,128)(2,1)S(1)} %get-tuple-element.1137, bf16[8,64]{1,0:T(8,128)(2,1)S(1)} %get-tuple-element.1135, ...), channel_id=1, replica_groups=mesh['seq'=32,'tp'=4] {'seq'}, use_global_device_ids=true, to_apply=%region_111.112 | all-reduce | flops 2048 | bytes 8192 | tf_op jit(solution)/shard_map/psum | solution.py:192
  1289.0 114.6 %all-reduce.32.cloned.1.call-done = (bf16[8,64,64]{2,1,0:T(8,128)(2,1)}, bf16[8,64,64]{2,1,0:T(8,128)(2,1)}, bf16[8,64,64]{2,1,0:T(8,128)(2,1)}, bf16[8,64,64]{2,1,0:T(8,128)(2,1)}) async-done(((bf16[8,64,64]{2,1,0:T(8,128)(2,1)}, bf16[8,64,64]{2,1,0:T(8,128)(2,1)}, bf16[8,64,64]{2,1,0:T(8,128)(2,1)}, bf16[8,64,64]{2,1,0:T(8,128)(2,1)}), (bf16[8,64,64]{2,1,0:T(8,128)(2,1)}, bf16[8,64,64]{2,1,0:T(8,128)(2,1)}, ...) | async-done | bytes 262160 | tf_op jit(solution)/shard_map/psum | solution.py:193
  1416.2 151.2 %all-reduce.24.cloned.1.call-done = (f32[64,2048]{1,0:T(8,128)}, f32[64,2048]{1,0:T(8,128)}, f32[64,2048]{1,0:T(8,128)}, f32[64,2048]{1,0:T(8,128)}) async-done(((f32[64,2048]{1,0:T(8,128)}, f32[64,2048]{1,0:T(8,128)}, f32[64,2048]{1,0:T(8,128)}, f32[64,2048]{1,0:T(8,128)}), (f32[64,2048]{1,0:T(8,128)}, f32[64,2048]{1,0:T(8,128)}, f32[64,2048]{1,0:T(8,128)}, ...) | async-done | bytes 2097168 | tf_op jit(solution)/shard_map/psum | solution.py:60
  (896 shorter events, 328.4 us)
Async XLA Ops:
  6.5 161.8 %all-reduce.22.cloned.1.call-start = ((), (), s32[]{:S(2)}) async-start(), calls=%async_computation | async-start | bytes 4194304 | tf_op jit(solution)/shard_map/psum | solution.py:60
  16.1 283.9 %all-reduce.30.cloned.1.call-start = ((), (), s32[]{:S(2)}) async-start(), calls=%async_computation.4 | async-start | bytes 10485760 | tf_op jit(solution)/shard_map/psum | solution.py:141
  186.4 518.4 %all-reduce.34.cloned.1.call-start = ((), (), s32[]{:S(2)}) async-start(), calls=%async_computation.6 | async-start | bytes 1048576 | tf_op jit(solution)/shard_map/psum | solution.py:193
  405.6 184.3 %copy-start.102 = (f32[8,64]{1,0:T(8,128)S(1)}, f32[8,64]{1,0:T(8,128)}, u32[]{:S(2)}) copy-start(f32[8,64]{1,0:T(8,128)} %copy-done.101) | copy-start | bytes 6148
  405.6 184.3 %copy-start.114 = (f32[8,64]{1,0:T(8,128)S(1)}, f32[8,64]{1,0:T(8,128)}, u32[]{:S(2)}) copy-start(f32[8,64]{1,0:T(8,128)} %get-tuple-element.1294) | copy-start | bytes 6148
  405.6 184.3 %copy-start.94 = (f32[8,64]{1,0:T(8,128)S(1)}, f32[8,64]{1,0:T(8,128)}, u32[]{:S(2)}) copy-start(f32[8,64]{1,0:T(8,128)} %copy-done.93) | copy-start | bytes 6148
  405.6 184.3 %copy-start.110 = (f32[8,64]{1,0:T(8,128)S(1)}, f32[8,64]{1,0:T(8,128)}, u32[]{:S(2)}) copy-start(f32[8,64]{1,0:T(8,128)} %get-tuple-element.1292) | copy-start | bytes 6148
  405.7 184.4 %copy-start.98 = (f32[8,64]{1,0:T(8,128)S(1)}, f32[8,64]{1,0:T(8,128)}, u32[]{:S(2)}) copy-start(f32[8,64]{1,0:T(8,128)} %copy-done.97) | copy-start | bytes 6148
  405.7 184.4 %copy-start.112 = (f32[8,64]{1,0:T(8,128)S(1)}, f32[8,64]{1,0:T(8,128)}, u32[]{:S(2)}) copy-start(f32[8,64]{1,0:T(8,128)} %get-tuple-element.1290) | copy-start | bytes 6148
  405.7 184.5 %copy-start.96 = (f32[8,64]{1,0:T(8,128)S(1)}, f32[8,64]{1,0:T(8,128)}, u32[]{:S(2)}) copy-start(f32[8,64]{1,0:T(8,128)} %copy-done.95) | copy-start | bytes 6148
  405.7 184.5 %copy-start.111 = (f32[8,64]{1,0:T(8,128)S(1)}, f32[8,64]{1,0:T(8,128)}, u32[]{:S(2)}) copy-start(f32[8,64]{1,0:T(8,128)} %get-tuple-element.1288) | copy-start | bytes 6148
  405.7 299.1 %copy-start.65 = (f32[8,64,1,64]{3,2,1,0:T(1,128)S(1)}, f32[8,64,1,64]{3,2,1,0:T(1,128)}, u32[]{:S(2)}) copy-start(f32[8,64,1,64]{3,2,1,0:T(1,128)} %fusion.150) | copy-start | bytes 393220
  407.6 298.8 %copy-start.64 = (f32[8,64,1,64]{3,2,1,0:T(1,128)S(1)}, f32[8,64,1,64]{3,2,1,0:T(1,128)}, u32[]{:S(2)}) copy-start(f32[8,64,1,64]{3,2,1,0:T(1,128)} %fusion.158) | copy-start | bytes 393220
  518.3 189.5 %copy-start.63 = (f32[8,64,1,64]{3,2,1,0:T(1,128)S(1)}, f32[8,64,1,64]{3,2,1,0:T(1,128)}, u32[]{:S(2)}) copy-start(f32[8,64,1,64]{3,2,1,0:T(1,128)} %fusion.166) | copy-start | bytes 393220
  590.1 278.7 %all-reduce.26.cloned.1.call-start = ((), (), s32[]{:S(2)}) async-start(), calls=%async_computation.2 | async-start | bytes 4194304 | tf_op jit(solution)/shard_map/psum | solution.py:60
  717.6 278.2 %all-reduce.28.cloned.1.call-start = ((), (), s32[]{:S(2)}) async-start(), calls=%async_computation.3 | async-start | bytes 10485760 | tf_op jit(solution)/shard_map/psum | solution.py:141
  882.3 521.2 %all-reduce.32.cloned.1.call-start = ((), (), s32[]{:S(2)}) async-start(), calls=%async_computation.5 | async-start | bytes 1048576 | tf_op jit(solution)/shard_map/psum | solution.py:193
  1104.3 182.7 %copy-start.106 = (f32[8,64]{1,0:T(8,128)S(1)}, f32[8,64]{1,0:T(8,128)}, u32[]{:S(2)}) copy-start(f32[8,64]{1,0:T(8,128)} %copy-done.105) | copy-start | bytes 6148
  1104.3 182.7 %copy-start.116 = (f32[8,64]{1,0:T(8,128)S(1)}, f32[8,64]{1,0:T(8,128)}, u32[]{:S(2)}) copy-start(f32[8,64]{1,0:T(8,128)} %get-tuple-element.1284) | copy-start | bytes 6148
  1104.3 182.7 %copy-start.104 = (f32[8,64]{1,0:T(8,128)S(1)}, f32[8,64]{1,0:T(8,128)}, u32[]{:S(2)}) copy-start(f32[8,64]{1,0:T(8,128)} %copy-done.103) | copy-start | bytes 6148
  1104.3 182.7 %copy-start.115 = (f32[8,64]{1,0:T(8,128)S(1)}, f32[8,64]{1,0:T(8,128)}, u32[]{:S(2)}) copy-start(f32[8,64]{1,0:T(8,128)} %get-tuple-element.1282) | copy-start | bytes 6148
  1215.3 188.3 %copy-start.66 = (f32[8,64,1,64]{3,2,1,0:T(1,128)S(1)}, f32[8,64,1,64]{3,2,1,0:T(1,128)}, u32[]{:S(2)}) copy-start(f32[8,64,1,64]{3,2,1,0:T(1,128)} %fusion.162) | copy-start | bytes 393220
  1217.6 187.4 %copy-start.67 = (f32[8,64,1,64]{3,2,1,0:T(1,128)S(1)}, f32[8,64,1,64]{3,2,1,0:T(1,128)}, u32[]{:S(2)}) copy-start(f32[8,64,1,64]{3,2,1,0:T(1,128)} %fusion.154) | copy-start | bytes 393220
  1288.9 278.5 %all-reduce.24.cloned.1.call-start = ((), (), s32[]{:S(2)}) async-start(), calls=%async_computation.1 | async-start | bytes 4194304 | tf_op jit(solution)/shard_map/psum | solution.py:60
  (155 other events, 1882.5 us)
Sparse Core Ops, SparseCore 0:
  16.3 152.0 all-reduce.21
  186.6 113.4 all-reduce.29
  590.2 114.5 all-reduce.33
  717.7 151.0 all-reduce.25
  882.5 113.2 all-reduce.27
  1289.0 114.5 all-reduce.31
  1416.3 151.0 all-reduce.23
where the time goes:
time: 1590 us; the launch traced here: 1580 us
  waiting for transfers between devices  852 us (54%)
  blocking collectives  353 us (22%)
  local copies, waits for them, and re-layouts  138 us (9%)
  matrix products  134 us (8%)
  other arithmetic  84.3 us (5%)
    psum x3, waiting for transfers between devices, full_total(): return lax.psum(values, ('seq', 'tp'))  441 us
    psum x2, waiting for transfers between devices, per_device(): lax.psum((part_out * factor[..., None]).astype(jnp.bfloat16), 'seq')  229 us
    pmax x2, blocking collectives, per_device(): cache_max = lax.pmax(part_max, 'seq')  216 us
    psum x2, waiting for transfers between devices, per_device(): attention_proj, fc1_all = lax.psum((part_proj, part_fc1), 'seq')  182 us
    psum x2, blocking collectives, per_device(): lax.psum((part_sum * factor).astype(jnp.bfloat16), 'seq')  137 us
    dot_general x32, matrix products, cache_step(): jnp.einsum('hrs,shd->hrd', weights.astype(jnp.bfloat16), value_block, pre...  44.8 us
  transfers between devices with their start and end apart: 7, of which 7 were waited for; matrix products, arithmetic and copies ran while one was open for 4% of the time, Pallas kernels for 0%

commit v1 on v0

v1 whole, which is shorter than its diff:
```python
import functools
import math

import jax
import jax.numpy as jnp
from jax import lax
from jax.experimental import pallas as pl
from jax.experimental.pallas import tpu as pltpu
from jax.sharding import PartitionSpec as P

HEADS = 32
HEAD_DIM = 64
ROT = 32
LAYERS = 2
BLOCK = 128
SPAN = 512
MESH_IDS = pl.DeviceIdType.MESH

very_negative = -1e30


def layer_norm(values, gain_row, bias_row):
    average = jnp.mean(values, axis=-1, keepdims=True)
    centred = values - average
    variance = jnp.mean(centred * centred, axis=-1, keepdims=True)
    return centred * lax.rsqrt(variance + 1e-05) * gain_row + bias_row


def rotary(values, positions):
    half_width = ROT // 2
    frequency = jnp.exp(
        jnp.arange(half_width, dtype=jnp.float32) * (-2.0 * math.log(10000.0) / ROT)
    )
    angles = positions.astype(jnp.float32)[:, None] * frequency[None, :]
    cosine = jnp.cos(angles)[:, None, :]
    sine_part = jnp.sin(angles)[:, None, :]
    low_half = values[..., :half_width]
    high_half = values[..., half_width:ROT]
    return jnp.concatenate(
        [
            low_half * cosine - high_half * sine_part,
            high_half * cosine + low_half * sine_part,
            values[..., ROT:],
        ],
        axis=-1,
    )


def _group_ids(whole, tp_count):
    seq_index = lax.axis_index("seq")
    tp_index = lax.axis_index("tp")
    if whole:
        me = seq_index * tp_count + tp_index

        def peer(j):
            return (j // tp_count, j % tp_count)

    else:
        me = seq_index

        def peer(j):
            return (j, tp_index)

    return me, peer


def _rcopy(src, dst, send_sem, recv_sem, device):
    return pltpu.make_async_remote_copy(
        src_ref=src,
        dst_ref=dst,
        send_sem=send_sem,
        recv_sem=recv_sem,
        device_id=device,
        device_id_type=MESH_IDS,
    )


def _allreduce_kernel(n, whole, tp_count, x_ref, o_ref, rs_buf, ag_buf, s1, r1, s2, r2):
    me, peer = _group_ids(whole, tp_count)

    def start_scatter(i, carry):
        j = lax.rem(me + i, n)
        _rcopy(x_ref.at[j], rs_buf.at[me], s1.at[j], r1.at[me], peer(j)).start()
        return carry

    lax.fori_loop(1, n, start_scatter, 0)

    def gather_sum(i, acc):
        j = lax.rem(me + i, n)
        _rcopy(x_ref.at[j], rs_buf.at[j], s1.at[j], r1.at[j], peer(j)).wait_recv()
        return acc + rs_buf[j].astype(jnp.float32)

    total = lax.fori_loop(1, n, gather_sum, x_ref[me].astype(jnp.float32))
    ag_buf[me] = total.astype(ag_buf.dtype)

    def start_gather(i, carry):
        j = lax.rem(me + i, n)
        _rcopy(ag_buf.at[me], ag_buf.at[me], s2.at[j], r2.at[me], peer(j)).start()
        return carry

    lax.fori_loop(1, n, start_gather, 0)

    def finish(i, carry):
        j = lax.rem(me + i, n)
        _rcopy(ag_buf.at[j], ag_buf.at[j], s2.at[j], r2.at[j], peer(j)).wait_recv()
        _rcopy(x_ref.at[j], rs_buf.at[me], s1.at[j], r1.at[me], peer(j)).wait_send()
        _rcopy(ag_buf.at[me], ag_buf.at[me], s2.at[j], r2.at[me], peer(j)).wait_send()
        return carry

    lax.fori_loop(1, n, finish, 0)
    o_ref[...] = ag_buf[...]


def allreduce(x, whole, tp_count):
    n = x.shape[0]
    return pl.pallas_call(
        functools.partial(_allreduce_kernel, n, whole, tp_count),
        out_shape=jax.ShapeDtypeStruct(x.shape, x.dtype),
        in_specs=[pl.BlockSpec(memory_space=pltpu.VMEM)],
        out_specs=pl.BlockSpec(memory_space=pltpu.VMEM),
        scratch_shapes=[
            pltpu.VMEM(x.shape, x.dtype),
            pltpu.VMEM(x.shape, x.dtype),
            pltpu.SemaphoreType.DMA((n,)),
            pltpu.SemaphoreType.DMA((n,)),
            pltpu.SemaphoreType.DMA((n,)),
            pltpu.SemaphoreType.DMA((n,)),
        ],
        compiler_params=pltpu.CompilerParams(has_side_effects=True),
    )(x)


def _all_to_all_kernel(n, whole, tp_count, x_ref, o_ref, buf, s1, r1):
    me, peer = _group_ids(whole, tp_count)

    def start(i, carry):
        j = lax.rem(me + i, n)
        _rcopy(x_ref.at[j], buf.at[me], s1.at[j], r1.at[me], peer(j)).start()
        return carry

    lax.fori_loop(1, n, start, 0)

    def finish(i, carry):
        j = lax.rem(me + i, n)
        _rcopy(x_ref.at[j], buf.at[j], s1.at[j], r1.at[j], peer(j)).wait_recv()
        _rcopy(x_ref.at[j], buf.at[me], s1.at[j], r1.at[me], peer(j)).wait_send()
        return carry

    lax.fori_loop(1, n, finish, 0)
    buf[me] = x_ref[me]
    o_ref[...] = buf[...]


def all_to_all(x, whole, tp_count):
    n = x.shape[0]
    return pl.pallas_call(
        functools.partial(_all_to_all_kernel, n, whole, tp_count),
        out_shape=jax.ShapeDtypeStruct(x.shape, x.dtype),
        in_specs=[pl.BlockSpec(memory_space=pltpu.VMEM)],
        out_specs=pl.BlockSpec(memory_space=pltpu.VMEM),
        scratch_shapes=[
            pltpu.VMEM(x.shape, x.dtype),
            pltpu.SemaphoreType.DMA((n,)),
            pltpu.SemaphoreType.DMA((n,)),
        ],
        compiler_params=pltpu.CompilerParams(has_side_effects=True),
    )(x)


def per_device(
    token_ids,
    embedding,
    group_of,
    prefix_len,
    tail_len,
    block_map,
    k_cache,
    v_cache,
    ln_gain,
    ln_bias,
    w_qkv,
    w_fc1,
    b_fc1,
    w_out,
    w_fc2,
):
    tp_count = lax.axis_size("tp")
    seq_count = lax.axis_size("seq")
    all_count = tp_count * seq_count
    seq_index = lax.axis_index("seq")
    tp_index = lax.axis_index("tp")
    requests = token_ids.shape[0]
    new_tokens = token_ids.shape[1]
    rows = requests * new_tokens
    groups = prefix_len.shape[0]
    heads_local = HEADS // tp_count
    width = embedding.shape[1]
    score_scale = 1.0 / math.sqrt(HEAD_DIM)

    vocab_rows = embedding.shape[0]
    first_row = (seq_index * tp_count + tp_index) * vocab_rows
    local_ids = token_ids.reshape(-1) - first_row
    inside = (local_ids >= 0) & (local_ids < vocab_rows)
    picked = jnp.take(embedding, jnp.clip(local_ids, 0, vocab_rows - 1), axis=0)
    picked = jnp.where(inside[:, None], picked, jnp.zeros_like(picked))
    start_states = allreduce(picked.reshape(all_count, -1, 128), True, tp_count)
    hidden_state = start_states.reshape(rows, width).astype(jnp.float32)

    group_hit = group_of[:, None] == jnp.arange(groups, dtype=jnp.int32)[None, :]
    shared_len = jnp.sum(jnp.where(group_hit, prefix_len[None, :], 0), axis=1)
    base_positions = shared_len + tail_len
    positions = (base_positions[:, None] + jnp.arange(new_tokens, dtype=jnp.int32)[None, :]).reshape(-1)
    seg_len = jnp.concatenate([prefix_len, tail_len])
    seg_count = seg_len.shape[0]
    blocks_local = block_map.shape[0]
    seg_blk = block_map[:, 0]
    rank_blk = block_map[:, 1]
    seg_hit = seg_blk[:, None] == jnp.arange(seg_count, dtype=jnp.int32)[None, :]
    len_blk = jnp.sum(jnp.where(seg_hit, seg_len[None, :], 0), axis=1)
    slot_positions = rank_blk[:, None] * BLOCK + jnp.arange(BLOCK, dtype=jnp.int32)[None, :]
    live_slot = ((seg_blk[:, None] >= 0) & (slot_positions < len_blk[:, None])).reshape(-1)
    seg_slot = jnp.broadcast_to(seg_blk[:, None], (blocks_local, BLOCK)).reshape(-1)
    own_tail = seg_slot[None, :] == (groups + jnp.arange(requests, dtype=jnp.int32))[:, None]
    own_prompt = seg_slot[None, :] == group_of[:, None]
    allowed = (own_tail | own_prompt) & live_slot[None, :]
    allowed = jnp.repeat(allowed, new_tokens, axis=0)
    step_count = allowed.shape[1] // SPAN
    allowed_steps = allowed.reshape(rows, step_count, SPAN).transpose(1, 0, 2)

    rows_local = w_qkv.shape[1]
    unit_count = w_fc2.shape[1]
    sub_width = w_out.shape[1]
    pieces = HEAD_DIM // sub_width
    my_head = seq_index // pieces
    my_piece = seq_index % pieces
    proj_width = 3 * heads_local * HEAD_DIM
    causal = (
        jnp.arange(new_tokens, dtype=jnp.int32)[None, :]
        <= jnp.arange(new_tokens, dtype=jnp.int32)[:, None]
    )
    for layer_index in range(LAYERS):
        normed = layer_norm(hidden_state, ln_gain[layer_index], ln_bias[layer_index]).astype(
            jnp.bfloat16
        )
        my_rows = lax.dynamic_slice_in_dim(normed, seq_index * rows_local, rows_local, 1)
        part_proj = jnp.dot(
            my_rows,
            w_qkv[layer_index].reshape(rows_local, -1),
            preferred_element_type=jnp.float32,
        )
        part_fc1 = jnp.dot(my_rows, w_fc1[layer_index], preferred_element_type=jnp.float32)
        joined = jnp.concatenate([part_proj, part_fc1], axis=1)
        joined = allreduce(joined.reshape(seq_count, rows // seq_count, -1), False, tp_count)
        joined = joined.reshape(rows, -1)
        attention_proj = joined[:, :proj_width]
        fc1_all = joined[:, proj_width:]
        pre_act = lax.dynamic_slice_in_dim(fc1_all, seq_index * unit_count, unit_count, 1)
        pre_act = (
            pre_act
            + lax.dynamic_slice_in_dim(b_fc1[layer_index], seq_index * unit_count, unit_count, 0)[
                None, :
            ]
        )
        activated = jax.nn.gelu(pre_act, approximate=True).astype(jnp.bfloat16)
        attention_proj = attention_proj.reshape(rows, 3, heads_local, HEAD_DIM)
        queries = rotary(attention_proj[:, 0], positions).astype(jnp.bfloat16)
        key_rows = rotary(attention_proj[:, 1], positions).astype(jnp.bfloat16)
        value_rows = attention_proj[:, 2].astype(jnp.bfloat16)
        key_steps = k_cache[layer_index].reshape(step_count, SPAN, heads_local, HEAD_DIM)
        value_steps = v_cache[layer_index].reshape(step_count, SPAN, heads_local, HEAD_DIM)

        def cache_step(carry, inputs):
            run_max, run_sum, run_out = carry
            key_block, value_block, allow_block = inputs
            scores = (
                jnp.einsum("rhd,shd->hrs", queries, key_block, preferred_element_type=jnp.float32)
                * score_scale
            )
            scores = jnp.where(allow_block[None], scores, very_negative)
            next_max = jnp.maximum(run_max, jnp.max(scores, axis=2))
            weights = jnp.where(allow_block[None], jnp.exp(scores - next_max[..., None]), 0.0)
            shrink = jnp.exp(run_max - next_max)
            next_sum = run_sum * shrink + jnp.sum(weights, axis=2)
            next_out = run_out * shrink[..., None] + jnp.einsum(
                "hrs,shd->hrd",
                weights.astype(jnp.bfloat16),
                value_block,
                preferred_element_type=jnp.float32,
            )
            return ((next_max, next_sum, next_out), None)

        start_carry = (
            jnp.full((heads_local, rows), very_negative, jnp.float32),
            jnp.zeros((heads_local, rows), jnp.float32),
            jnp.zeros((heads_local, rows, HEAD_DIM), jnp.float32),
        )
        (part_max, part_sum, part_out), unused = lax.scan(
            cache_step, start_carry, (key_steps, value_steps, allowed_steps)
        )
        out_pieces = (
            part_out.reshape(heads_local, rows, pieces, sub_width)
            .transpose(0, 2, 3, 1)
            .reshape(heads_local * pieces, sub_width, rows)
        )
        max_rows = jnp.repeat(part_max, pieces, axis=0)[:, None, :]
        sum_rows = jnp.repeat(part_sum, pieces, axis=0)[:, None, :]
        pad_rows = jnp.zeros((heads_local * pieces, 6, rows), jnp.float32)
        message = jnp.concatenate([out_pieces, max_rows, sum_rows, pad_rows], axis=1)
        received = all_to_all(message, False, tp_count)
        got_out = received[:, :sub_width, :]
        got_max = received[:, sub_width, :]
        got_sum = received[:, sub_width + 1, :]

        q4 = queries.reshape(requests, new_tokens, heads_local, HEAD_DIM)
        k4 = key_rows.reshape(requests, new_tokens, heads_local, HEAD_DIM)
        v4 = value_rows.reshape(requests, new_tokens, heads_local, HEAD_DIM)
        q_h = lax.dynamic_index_in_dim(q4, my_head, 2, keepdims=False)
        k_h = lax.dynamic_index_in_dim(k4, my_head, 2, keepdims=False)
        v_h = lax.dynamic_index_in_dim(v4, my_head, 2, keepdims=False)
        v_h = lax.dynamic_slice_in_dim(v_h, my_piece * sub_width, sub_width, 2)
        fresh_scores = (
            jnp.einsum("rtd,rud->rtu", q_h, k_h, preferred_element_type=jnp.float32) * score_scale
        )
        fresh_scores = jnp.where(causal[None], fresh_scores, very_negative)
        fresh_max = jnp.max(fresh_scores, axis=2)
        fresh_weights = jnp.where(causal[None], jnp.exp(fresh_scores - fresh_max[..., None]), 0.0)
        fresh_sum = jnp.sum(fresh_weights, axis=2)
        fresh_out = jnp.einsum(
            "rtu,rud->rtd",
            fresh_weights.astype(jnp.bfloat16),
            v_h,
            preferred_element_type=jnp.float32,
        )
        fresh_max = fresh_max.reshape(rows)
        fresh_sum = fresh_sum.reshape(rows)
        fresh_out = fresh_out.reshape(rows, sub_width)

        top = jnp.maximum(jnp.max(got_max, axis=0), fresh_max)
        scale_cache = jnp.exp(got_max - top[None, :])
        scale_fresh = jnp.exp(fresh_max - top)
        denom = jnp.sum(got_sum * scale_cache, axis=0) + fresh_sum * scale_fresh
        numer = jnp.sum(got_out * scale_cache[:, None, :], axis=0).T + fresh_out * scale_fresh[:, None]
        my_cols = (numer / denom[:, None]).astype(jnp.bfloat16)

        update = jnp.dot(my_cols, w_out[layer_index], preferred_element_type=jnp.float32)
        update = update + jnp.dot(activated, w_fc2[layer_index], preferred_element_type=jnp.float32)
        update = allreduce(update.reshape(all_count, -1, 128), True, tp_count)
        hidden_state = hidden_state + update.reshape(rows, width)
    return hidden_state.reshape(requests, new_tokens, width)


def solution(mesh):
    in_specs = (
        P(),
        P(("seq", "tp"), None),
        P(),
        P(),
        P(),
        P("seq", None),
        P(None, "seq", "tp"),
        P(None, "seq", "tp"),
        P(),
        P(),
        P(None, "seq", None, "tp"),
        P(None, "seq", "tp"),
        P(None, "tp"),
        P(None, ("tp", "seq"), None),
        P(None, ("tp", "seq"), None),
    )
    out_specs = P()
    return jax.shard_map(
        per_device, mesh=mesh, in_specs=in_specs, out_specs=out_specs, check_vma=False
    )
```

time: 1590 us -> 816 us (0.51)
  waiting for transfers between devices: 852 us -> 0 us
  Pallas kernels: 0 us -> 594 us
  blocking collectives: 353 us -> 0 us
  matrix products: 134 us -> 45 us
  other arithmetic: 84.3 us -> 49.9 us
  local copies, waits for them, and re-layouts: 138 us -> 116 us
    psum x7 -> x0, waiting for transfers between devices: 852 us -> none  [the longest x3 441 us: full_total(): return lax.psum(values, ('seq', 'tp'))]
    pallas_call x0 -> x7, Pallas kernels: none -> 594 us  [the longest x5 545 us: allreduce(): pl.pallas_call(functools.partial(_allreduce_kernel, n, whole, tp_count),...]
    pmax x2 -> x0, blocking collectives: 216 us -> none  [per_device(): cache_max = lax.pmax(part_max, 'seq')]
    psum x2 -> x0, blocking collectives: 137 us -> none  [per_device(): lax.psum((part_sum * factor).astype(jnp.bfloat16), 'seq')]
    dot_general x16 -> x4, matrix products: 33.2 us -> 0.79 us  [the longest x2 0.4 us: per_device(): jnp.einsum('rtd,rud->rtu', q_h, k_h, preferred_element_type=jnp.float32)]
    dot_general x32 -> x8, matrix products: 44.8 us -> 18.4 us  [cache_step(): jnp.einsum('hrs,shd->hrd', weights.astype(jnp.bfloat16), value_block, pre...]
    convert_element_type x24 -> x0, other arithmetic: 25.7 us -> none  [the longest x8 14 us: per_device(): fresh_weights.astype(jnp.bfloat16)]
  transfers between devices with their start and end apart: 7 -> 0, of which waited for: 7 -> 0; matrix products, arithmetic and copies ran while one was open for 4% -> 0% of each run, Pallas kernels for 0% -> 0%
where the time goes in v1:
time: 816 us; the launch traced here: 806 us
  Pallas kernels  594 us (73%)
  local copies, waits for them, and re-layouts  116 us (14%)
  other arithmetic  49.9 us (6%)
  matrix products  45 us (6%)
    pallas_call x5, Pallas kernels, allreduce(): pl.pallas_call(functools.partial(_allreduce_kernel, n, whole, tp_count),...  545 us
    pallas_call x2, Pallas kernels, all_to_all(): pl.pallas_call(functools.partial(_all_to_all_kernel, n, whole, tp_count),...  48.9 us
    unnamed x63, local copies, waits for them, and re-layouts  27.4 us
    dot_general x8, matrix products, cache_step(): jnp.einsum('hrs,shd->hrd', weights.astype(jnp.bfloat16), value_block, pre...  18.4 us

profile of v1, /device:TPU:25, one launch (start us, length us, event | category | flops | bytes accessed | tf_op | source)
XLA Modules:
  0.0 806.2 jit_solution(8303835542374897001)
XLA Ops:
  23.0 57.0 %shard_map.145 = bf16[128,32,128]{2,1,0:T(8,128)(2,1)} custom-call(bf16[128,32,128]{2,1,0:T(8,128)(2,1)} %select_select_fusion.x_ref), custom_call_target="tpu_custom_call" | custom-call | tf_op jit(solution)/shard_map/pallas_call | solution.py:116
  90.7 154.9 %shard_map.146 = f32[32,8,3584]{2,1,0:T(8,128)} custom-call(f32[32,8,3584]{2,1,0:T(8,128)} %maximum_bitcast_fusion.x_ref), custom_call_target="tpu_custom_call" | custom-call | tf_op jit(solution)/shard_map/pallas_call | solution.py:116
  262.0 2.9 fusion.57
  266.3 4.5 fusion.139
  270.8 6.2 reshape.439
  277.1 5.4 copy.325
  282.5 6.2 reshape.441
  288.7 5.5 copy.354
  294.2 4.5 fusion.138
  298.7 6.2 reshape.442
  304.9 5.5 copy.355
  310.4 6.2 reshape.440
  316.6 5.6 copy.326
  322.2 21.4 %while.30 = (s32[]{:T(128)}, f32[8,256]{1,0:T(8,128)S(1)}, f32[8,256]{1,0:T(8,128)S(1)}, f32[8,256,64]{1,2,0:T(8,128)S(1)}, pred[4,256,512]{1,2,0:T(8,128)(4,1)S...) while((s32[]{:T(128)}, f32[8,256]{1,0:T(8,128)S(1)}, ...), condition=%wide.region_9.10_spmd.clone, body=%wide.region_6.9_spmd.clone.sunk | while | flops 282470400 | bytes 15728773 | solution.py:297
  344.7 26.6 %shard_map.147 = f32[32,24,256]{2,1,0:T(8,128)} custom-call(f32[32,24,256]{2,1,0:T(8,128)} %maximum_maximum_fusion.x_ref), custom_call_target="tpu_custom_call" | custom-call | tf_op jit(solution)/shard_map/pallas_call | solution.py:156
  376.0 2.8 reshape.419.x_ref
  378.7 90.7 %shard_map.148 = f32[128,32,128]{2,1,0:T(8,128)} custom-call(f32[128,32,128]{2,1,0:T(8,128)} %reshape.419.x_ref), custom_call_target="tpu_custom_call" | custom-call | tf_op jit(solution)/shard_map/pallas_call | solution.py:116
  474.9 2.7 reshape.420
  482.8 151.6 %shard_map.149 = f32[32,8,3584]{2,1,0:T(8,128)} custom-call(f32[32,8,3584]{2,1,0:T(8,128)} %maximum_bitcast_fusion.1.x_ref), custom_call_target="tpu_custom_call" | custom-call | tf_op jit(solution)/shard_map/pallas_call | solution.py:116
  642.1 24.3 %while.31 = (s32[]{:T(128)}, f32[8,256]{1,0:T(8,128)S(1)}, f32[8,256]{1,0:T(8,128)S(1)}, f32[8,256,64]{1,2,0:T(8,128)}, pred[4,256,512]{1,2,0:T(8,128)(4,1)S(1)}...) while((s32[]{:T(128)}, f32[8,256]{1,0:T(8,128)S(1)}, ...), condition=%wide.region_22.23_spmd.clone, body=%wide.region_19.22_spmd.clone.sunk | while | flops 282470400 | bytes 19923132 | solution.py:297
  668.5 22.4 %shard_map.150 = f32[32,24,256]{2,1,0:T(8,128)} custom-call(f32[32,24,256]{2,1,0:T(8,128)} %maximum_maximum_fusion.1.x_ref), custom_call_target="tpu_custom_call" | custom-call | tf_op jit(solution)/shard_map/pallas_call | solution.py:156
  708.2 90.6 %shard_map.151 = f32[128,32,128]{2,1,0:T(8,128)} custom-call(f32[128,32,128]{2,1,0:T(8,128)} %reshape.429.x_ref), custom_call_target="tpu_custom_call" | custom-call | tf_op jit(solution)/shard_map/pallas_call | solution.py:116
  798.9 4.3 fusion.40
  803.1 2.9 add.295
  (310 shorter events, 139.1 us)
Async XLA Ops:
  0.0 18.6 %copy-start = (bf16[400,2048]{1,0:T(8,128)(2,1)S(1)}, bf16[400,2048]{1,0:T(8,128)(2,1)}, u32[]{:S(2)}) copy-start(bf16[400,2048]{1,0:T(8,128)(2,1)} %param.20) | copy-start | bytes 4915204
  80.0 2.5 copy-start.2
  250.7 2.4 copy-start.14
  250.7 2.4 copy-start.16
  262.0 3.3 copy-start.22
  262.0 4.0 copy-start.13
  316.6 5.6 copy-start.9
  316.6 5.6 copy-start.11
  322.2 21.5 %copy-start.23 = (f32[24]{0:T(128)S(1)}, f32[24]{0:T(128)}, u32[]{:S(2)}) copy-start(f32[24]{0:T(128)} %pad.24.clone) | copy-start | bytes 292
  343.5 30.1 %copy-start.18 = (bf16[2,16,2048]{2,1,0:T(8,128)(2,1)S(1)}, bf16[2,16,2048]{2,1,0:T(8,128)(2,1)}, u32[]{:S(2)}) copy-start(bf16[2,16,2048]{2,1,0:T(8,128)(2,1)} %param.32) | copy-start | bytes 393220
  344.7 29.4 %copy-start.5 = (bf16[2,64,2048]{2,1,0:T(8,128)(2,1)S(1)}, bf16[2,64,2048]{2,1,0:T(8,128)(2,1)}, u32[]{:S(2)}) copy-start(bf16[2,64,2048]{2,1,0:T(8,128)(2,1)} %param.33) | copy-start | bytes 1572868
  344.7 29.4 %copy-start.27 = (f32[64]{0:T(128)S(1)}, f32[64]{0:T(128)}, u32[]{:S(2)}) copy-start(f32[64]{0:T(128)} %get-tuple-element.335) | copy-start | bytes 772
  474.9 2.7 copy-start.24
  474.9 2.7 copy-start.25
  639.5 2.4 copy-start.15
  639.5 2.4 copy-start.17
  697.8 4.8 copy-start.20
  697.8 4.9 copy-start.3
  698.7 2.9 copy-start.21
  698.7 4.1 copy-start.12
  698.8 4.4 copy-start.19
  701.6 2.1 copy-start.6
  701.6 2.1 copy-start.26
  798.8 7.2 copy-start.1
  (10 other events, 10.3 us)

commit v2 on v1

--- a/solution.py
+++ b/solution.py
@@ -233,28 +233,33 @@
     pieces = HEAD_DIM // sub_width
     my_head = seq_index // pieces
     my_piece = seq_index % pieces
-    proj_width = 3 * heads_local * HEAD_DIM
     causal = (
         jnp.arange(new_tokens, dtype=jnp.int32)[None, :]
         <= jnp.arange(new_tokens, dtype=jnp.int32)[:, None]
     )
+
+    head_of = jnp.arange(seq_count, dtype=jnp.int32) // pieces
+    qkv_heads = w_qkv.reshape(LAYERS, rows_local, 3, heads_local, HEAD_DIM)
+    qkv_part = jnp.take(qkv_heads, head_of, axis=3)
+    qkv_part = qkv_part.transpose(3, 0, 1, 2, 4).reshape(seq_count, LAYERS, rows_local, 3 * HEAD_DIM)
+    fc1_part = w_fc1.reshape(LAYERS, rows_local, seq_count, unit_count).transpose(2, 0, 1, 3)
+    message = jnp.concatenate([qkv_part, fc1_part], axis=-1)
+    cols_mine = message.shape[-1]
+    got_w = all_to_all(message.reshape(seq_count, LAYERS * rows_local, cols_mine), False, tp_count)
+    w_mine = (
+        got_w.reshape(seq_count, LAYERS, rows_local, cols_mine)
+        .transpose(1, 0, 2, 3)
+        .reshape(LAYERS, seq_count * rows_local, cols_mine)
+    )
     for layer_index in range(LAYERS):
         normed = layer_norm(hidden_state, ln_gain[layer_index], ln_bias[layer_index]).astype(
             jnp.bfloat16
         )
-        my_rows = lax.dynamic_slice_in_dim(normed, seq_index * rows_local, rows_local, 1)
-        part_proj = jnp.dot(
-            my_rows,
-            w_qkv[layer_index].reshape(rows_local, -1),
-            preferred_element_type=jnp.float32,
-        )
-        part_fc1 = jnp.dot(my_rows, w_fc1[layer_index], preferred_element_type=jnp.float32)
-        joined = jnp.concatenate([part_proj, part_fc1], axis=1)
-        joined = allreduce(joined.reshape(seq_count, rows // seq_count, -1), False, tp_count)
-        joined = joined.reshape(rows, -1)
-        attention_proj = joined[:, :proj_width]
-        fc1_all = joined[:, proj_width:]
-        pre_act = lax.dynamic_slice_in_dim(fc1_all, seq_index * unit_count, unit_count, 1)
+        local = jnp.dot(normed, w_mine[layer_index], preferred_element_type=jnp.float32)
+        q_h = rotary(local[:, None, 0:HEAD_DIM], positions)[:, 0].astype(jnp.bfloat16)
+        k_h = rotary(local[:, None, HEAD_DIM : 2 * HEAD_DIM], positions)[:, 0].astype(jnp.bfloat16)
+        v_h = local[:, 2 * HEAD_DIM : 3 * HEAD_DIM].astype(jnp.bfloat16)
+        pre_act = local[:, 3 * HEAD_DIM :]
         pre_act = (
             pre_act
             + lax.dynamic_slice_in_dim(b_fc1[layer_index], seq_index * unit_count, unit_count, 0)[
@@ -262,10 +267,13 @@
             ]
         )
         activated = jax.nn.gelu(pre_act, approximate=True).astype(jnp.bfloat16)
-        attention_proj = attention_proj.reshape(rows, 3, heads_local, HEAD_DIM)
-        queries = rotary(attention_proj[:, 0], positions).astype(jnp.bfloat16)
-        key_rows = rotary(attention_proj[:, 1], positions).astype(jnp.bfloat16)
-        value_rows = attention_proj[:, 2].astype(jnp.bfloat16)
+        q_piece = lax.dynamic_slice_in_dim(q_h, my_piece * sub_width, sub_width, 1).T
+        q_all = all_to_all(jnp.broadcast_to(q_piece[None], (seq_count,) + q_piece.shape), False, tp_count)
+        queries = (
+            q_all.reshape(heads_local, pieces, sub_width, rows)
+            .transpose(3, 0, 1, 2)
+            .reshape(rows, heads_local, HEAD_DIM)
+        )
         key_steps = k_cache[layer_index].reshape(step_count, SPAN, heads_local, HEAD_DIM)
         value_steps = v_cache[layer_index].reshape(step_count, SPAN, heads_local, HEAD_DIM)
 
@@ -311,13 +319,10 @@
         got_max = received[:, sub_width, :]
         got_sum = received[:, sub_width + 1, :]
 
-        q4 = queries.reshape(requests, new_tokens, heads_local, HEAD_DIM)
-        k4 = key_rows.reshape(requests, new_tokens, heads_local, HEAD_DIM)
-        v4 = value_rows.reshape(requests, new_tokens, heads_local, HEAD_DIM)
-        q_h = lax.dynamic_index_in_dim(q4, my_head, 2, keepdims=False)
-        k_h = lax.dynamic_index_in_dim(k4, my_head, 2, keepdims=False)
-        v_h = lax.dynamic_index_in_dim(v4, my_head, 2, keepdims=False)
-        v_h = lax.dynamic_slice_in_dim(v_h, my_piece * sub_width, sub_width, 2)
+        q_h = q_h.reshape(requests, new_tokens, HEAD_DIM)
+        k_h = k_h.reshape(requests, new_tokens, HEAD_DIM)
+        v_h = lax.dynamic_slice_in_dim(v_h, my_piece * sub_width, sub_width, 1)
+        v_h = v_h.reshape(requests, new_tokens, sub_width)
         fresh_scores = (
             jnp.einsum("rtd,rud->rtu", q_h, k_h, preferred_element_type=jnp.float32) * score_scale
         )

time: 816 us -> 610 us (0.75)
  Pallas kernels: 594 us -> 368 us
  matrix products: 45 us -> 63.5 us
  other arithmetic: 49.9 us -> 62 us
  local copies, waits for them, and re-layouts: 116 us -> 104 us
    pallas_call x5 -> x3, Pallas kernels: 545 us -> 238 us  [allreduce(): pl.pallas_call(functools.partial(_allreduce_kernel, n, whole, tp_count),...]
    pallas_call x2 -> x5, Pallas kernels: 48.9 us -> 129 us  [all_to_all(): pl.pallas_call(functools.partial(_all_to_all_kernel, n, whole, tp_count),...]
    reduce_sum x8, other arithmetic: 8 us -> 26.7 us  [cache_step(): next_sum = run_sum * shrink + jnp.sum(weights, axis=2)]
    dot_general x8, matrix products: 15.2 us -> 30.5 us  [cache_step(): jnp.einsum('rhd,shd->hrs', queries, key_block, preferred_element_type=jnp...]
    concatenate x0 -> x4, local copies, waits for them, and re-layouts: none -> 13.8 us  [the longest x2 13.6 us: per_device(): message = jnp.concatenate([qkv_part, fc1_part], axis=-1)]
    another operation x11 -> x3, local copies, waits for them, and re-layouts: 9.39 us -> 0.02 us
    unnamed x63 -> x39, local copies, waits for them, and re-layouts: 27.4 us -> 23.7 us
where the time goes in v2:
time: 610 us; the launch traced here: 598 us
  Pallas kernels  368 us (60%)
  local copies, waits for them, and re-layouts  104 us (17%)
  matrix products  63.5 us (10%)
  other arithmetic  62 us (10%)
    pallas_call x3, Pallas kernels, allreduce(): pl.pallas_call(functools.partial(_allreduce_kernel, n, whole, tp_count),...  238 us
    pallas_call x5, Pallas kernels, all_to_all(): pl.pallas_call(functools.partial(_all_to_all_kernel, n, whole, tp_count),...  129 us
    dot_general x8, matrix products, cache_step(): jnp.einsum('rhd,shd->hrs', queries, key_block, preferred_element_type=jnp...  30.5 us
    reduce_sum x8, other arithmetic, cache_step(): next_sum = run_sum * shrink + jnp.sum(weights, axis=2)  26.7 us
    unnamed x39, local copies, waits for them, and re-layouts  23.7 us
    dot_general x8, matrix products, cache_step(): jnp.einsum('hrs,shd->hrd', weights.astype(jnp.bfloat16), value_block, pre...  22.1 us
    concatenate x2, local copies, waits for them, and re-layouts, per_device(): message = jnp.concatenate([qkv_part, fc1_part], axis=-1)  13.6 us
    another operation x2, local copies, waits for them, and re-layouts, per_device(): k_cache[layer_index].reshape(step_count, SPAN, heads_local, HEAD_DIM)  12.4 us

profile of v2, /device:TPU:25, one launch (start us, length us, event | category | flops | bytes accessed | tf_op | source)
XLA Modules:
  0.0 598.3 jit_solution(8230330274606180654)
XLA Ops:
  6.6 57.0 %shard_map.145 = bf16[128,32,128]{2,1,0:T(8,128)(2,1)} custom-call(bf16[128,32,128]{2,1,0:T(8,128)(2,1)} %select_select_fusion.x_ref), custom_call_target="tpu_custom_call" | custom-call | tf_op jit(solution)/shard_map/pallas_call | solution.py:116
  76.4 5.0 copy.294
  81.5 8.5 %reshape.566 = bf16[32,128,192]{2,1,0:T(8,128)(2,1)} reshape(bf16[32,2,64,3,64]{4,3,2,1,0:T(4,128)(2,1)} %copy.294) | data formatting | bytes 3145728 | tf_op jit(solution)/shard_map/concatenate | solution.py:246
  96.0 49.9 %shard_map.146 = bf16[32,128,256]{2,1,0:T(8,128)(2,1)} custom-call(bf16[32,128,256]{2,1,0:T(8,128)(2,1)} %pad_maximum_fusion.x_ref), custom_call_target="tpu_custom_call" | custom-call | tf_op jit(solution)/shard_map/pallas_call | solution.py:156
  151.6 18.5 %shard_map.147 = bf16[32,16,256]{2,1,0:T(8,128)(2,1)S(1)} custom-call(bf16[32,16,256]{2,1,0:T(8,128)(2,1)} %broadcast_in_dim.253.x_ref), custom_call_target="tpu_custom_call" | custom-call | tf_op jit(solution)/shard_map/pallas_call | solution.py:156
  173.3 4.5 fusion.148
  177.8 6.2 %reshape.565 = bf16[4,512,8,64]{3,2,1,0:T(8,128)(2,1)} reshape(bf16[1,2048,512]{2,1,0:T(8,128)(2,1)} %get-tuple-element.295) | data formatting | bytes 4194304 | tf_op jit(solution)/shard_map/reshape;squeeze | solution.py:277
  184.0 5.4 copy.261
  189.4 4.6 fusion.147
  194.0 6.2 %reshape.567 = bf16[4,512,8,64]{3,2,1,0:T(8,128)(2,1)} reshape(bf16[1,2048,512]{2,1,0:T(8,128)(2,1)} %get-tuple-element.294) | data formatting | bytes 4194304 | tf_op jit(solution)/shard_map/reshape;squeeze | solution.py:278
  200.2 5.5 copy.262
  205.7 38.4 %while.30 = (s32[]{:T(128)}, f32[8,256]{1,0:T(8,128)S(1)}, f32[8,256]{1,0:T(8,128)S(1)}, f32[8,256,64]{1,2,0:T(8,128)S(1)}, pred[4,256,512]{1,2,0:T(8,128)(4,1)S...) while((s32[]{:T(128)}, f32[8,256]{1,0:T(8,128)S(1)}, ...), condition=%wide.region_9.10_spmd.clone, body=%wide.region_6.9_spmd.clone.sunk | while | flops 282470400 | bytes 32507024 | solution.py:305
  245.4 23.6 %shard_map.148 = f32[32,24,256]{2,1,0:T(8,128)} custom-call(f32[32,24,256]{2,1,0:T(8,128)} %maximum_maximum_fusion.x_ref), custom_call_target="tpu_custom_call" | custom-call | tf_op jit(solution)/shard_map/pallas_call | solution.py:156
  280.3 90.6 %shard_map.149 = f32[128,32,128]{2,1,0:T(8,128)} custom-call(f32[128,32,128]{2,1,0:T(8,128)} %reshape.539.x_ref), custom_call_target="tpu_custom_call" | custom-call | tf_op jit(solution)/shard_map/pallas_call | solution.py:116
  376.8 4.1 add_convert_fusion
  387.2 13.9 %shard_map.150 = bf16[32,16,256]{2,1,0:T(8,128)(2,1)S(1)} custom-call(bf16[32,16,256]{2,1,0:T(8,128)(2,1)} %broadcast_in_dim.261.x_ref), custom_call_target="tpu_custom_call" | custom-call | tf_op jit(solution)/shard_map/pallas_call | solution.py:156
  401.2 6.2 %reshape.568 = bf16[4,512,8,64]{3,2,1,0:T(8,128)(2,1)} reshape(bf16[1,2048,512]{2,1,0:T(8,128)(2,1)} %get-tuple-element.296) | data formatting | bytes 4194304 | tf_op jit(solution)/shard_map/reshape;squeeze | solution.py:277
  407.4 5.4 copy.279
  412.8 6.2 %reshape.569 = bf16[4,512,8,64]{3,2,1,0:T(8,128)(2,1)} reshape(bf16[1,2048,512]{2,1,0:T(8,128)(2,1)} %get-tuple-element.293) | data formatting | bytes 4194304 | tf_op jit(solution)/shard_map/reshape;squeeze | solution.py:278
  419.0 5.5 copy.280
  424.4 42.0 %while.31 = (s32[]{:T(128)}, f32[8,256]{1,0:T(8,128)S(1)}, f32[8,256]{1,0:T(8,128)S(1)}, f32[8,256,64]{1,2,0:T(8,128)}, pred[4,256,512]{1,2,0:T(8,128)(4,1)S(1)}...) while((s32[]{:T(128)}, f32[8,256]{1,0:T(8,128)S(1)}, ...), condition=%wide.region_22.23_spmd.clone, body=%wide.region_19.22_spmd.clone.sunk | while | flops 282470400 | bytes 32507024 | solution.py:305
  468.6 23.4 %shard_map.151 = f32[32,24,256]{2,1,0:T(8,128)} custom-call(f32[32,24,256]{2,1,0:T(8,128)} %maximum_maximum_fusion.1.x_ref), custom_call_target="tpu_custom_call" | custom-call | tf_op jit(solution)/shard_map/pallas_call | solution.py:156
  500.3 90.6 %shard_map.152 = f32[128,32,128]{2,1,0:T(8,128)} custom-call(f32[128,32,128]{2,1,0:T(8,128)} %reshape.548.x_ref), custom_call_target="tpu_custom_call" | custom-call | tf_op jit(solution)/shard_map/pallas_call | solution.py:116
  590.9 4.2 fusion.50
  (285 shorter events, 151.7 us)
Async XLA Ops:
  0.0 1.4 copy-start
  2.8 0.9 copy-start.14
  63.7 2.5 copy-start.4
  63.7 4.3 copy-start.11
  63.7 4.4 copy-start.12
  68.1 2.8 copy-start.9
  81.5 8.5 %copy-start.7 = (bf16[2,64,2048]{2,1,0:T(8,128)(2,1)S(1)}, bf16[2,64,2048]{2,1,0:T(8,128)(2,1)}, u32[]{:S(2)}) copy-start(bf16[2,64,2048]{2,1,0:T(8,128)(2,1)} %param.30) | copy-start | bytes 1572868
  92.1 1.9 copy-start.5
  145.9 2.8 copy-start.6
  148.7 0.7 copy-start.18
  148.7 0.8 copy-start.17
  148.7 21.5 %copy-start.15 = (s32[16,2]{0,1:T(2,128)S(1)}, s32[16,2]{0,1:T(2,128)}, u32[]{:S(2)}) copy-start(s32[16,2]{0,1:T(2,128)} %param.24) | copy-start | bytes 388
  209.5 3.4 copy-start.2
  219.1 3.4 copy-start.2
  228.7 3.4 copy-start.2
  238.4 3.4 copy-start.2
  244.4 27.9 %copy-start.10 = (bf16[2,16,2048]{2,1,0:T(8,128)(2,1)S(1)}, bf16[2,16,2048]{2,1,0:T(8,128)(2,1)}, u32[]{:S(2)}) copy-start(bf16[2,16,2048]{2,1,0:T(8,128)(2,1)} %param.32) | copy-start | bytes 393220
  269.0 5.1 copy-start.13
  269.0 5.2 copy-start.8
  428.3 3.4 copy-start.3
  438.7 3.4 copy-start.3
  449.2 3.4 copy-start.3
  459.7 3.4 copy-start.3
  590.9 7.1 %copy-start.1 = (bf16[400,2048]{1,0:T(8,128)(2,1)S(1)}, bf16[400,2048]{1,0:T(8,128)(2,1)}, u32[]{:S(2)}) copy-start(bf16[400,2048]{1,0:T(8,128)(2,1)} %param.20) | copy-start | bytes 4915204
  (1 other events, 0.7 us)

commit v3 on v2

--- a/solution.py
+++ b/solution.py
@@ -224,8 +224,6 @@
     own_prompt = seg_slot[None, :] == group_of[:, None]
     allowed = (own_tail | own_prompt) & live_slot[None, :]
     allowed = jnp.repeat(allowed, new_tokens, axis=0)
-    step_count = allowed.shape[1] // SPAN
-    allowed_steps = allowed.reshape(rows, step_count, SPAN).transpose(1, 0, 2)
 
     rows_local = w_qkv.shape[1]
     unit_count = w_fc2.shape[1]
@@ -274,36 +272,39 @@
             .transpose(3, 0, 1, 2)
             .reshape(rows, heads_local, HEAD_DIM)
         )
-        key_steps = k_cache[layer_index].reshape(step_count, SPAN, heads_local, HEAD_DIM)
-        value_steps = v_cache[layer_index].reshape(step_count, SPAN, heads_local, HEAD_DIM)
-
-        def cache_step(carry, inputs):
-            run_max, run_sum, run_out = carry
-            key_block, value_block, allow_block = inputs
-            scores = (
-                jnp.einsum("rhd,shd->hrs", queries, key_block, preferred_element_type=jnp.float32)
-                * score_scale
+        head_cols = (
+            jnp.arange(heads_local * HEAD_DIM, dtype=jnp.int32)[None, :] // HEAD_DIM
+            == jnp.arange(heads_local, dtype=jnp.int32)[:, None]
+        )
+        q_block = jnp.where(
+            head_cols[:, None, :], queries.reshape(rows, heads_local * HEAD_DIM)[None], 0
+        ).astype(jnp.bfloat16)
+        scores = (
+            jnp.einsum(
+                "hrc,sc->hrs", q_block, k_cache[layer_index], preferred_element_type=jnp.float32
             )
-            scores = jnp.where(allow_block[None], scores, very_negative)
-            next_max = jnp.maximum(run_max, jnp.max(scores, axis=2))
-            weights = jnp.where(allow_block[None], jnp.exp(scores - next_max[..., None]), 0.0)
-            shrink = jnp.exp(run_max - next_max)
-            next_sum = run_sum * shrink + jnp.sum(weights, axis=2)
-            next_out = run_out * shrink[..., None] + jnp.einsum(
-                "hrs,shd->hrd",
-                weights.astype(jnp.bfloat16),
-                value_block,
-                preferred_element_type=jnp.float32,
-            )
-            return ((next_max, next_sum, next_out), None)
-
-        start_carry = (
-            jnp.full((heads_local, rows), very_negative, jnp.float32),
-            jnp.zeros((heads_local, rows), jnp.float32),
-            jnp.zeros((heads_local, rows, HEAD_DIM), jnp.float32),
-        )
-        (part_max, part_sum, part_out), unused = lax.scan(
-            cache_step, start_carry, (key_steps, value_steps, allowed_steps)
+            * score_scale
+        )
+        scores = jnp.where(allowed[None], scores, very_negative)
+        part_max = jnp.max(scores, axis=2)
+        weights = jnp.where(allowed[None], jnp.exp(scores - part_max[..., None]), 0.0)
+        part_sum = jnp.sum(weights, axis=2)
+        out_all = jnp.einsum(
+            "hrs,sc->hrc",
+            weights.astype(jnp.bfloat16),
+            v_cache[layer_index],
+            preferred_element_type=jnp.float32,
+        ).reshape(heads_local, rows, heads_local, HEAD_DIM)
+        part_out = jnp.sum(
+            jnp.where(
+                (
+                    jnp.arange(heads_local, dtype=jnp.int32)[:, None]
+                    == jnp.arange(heads_local, dtype=jnp.int32)[None, :]
+                )[:, None, :, None],
+                out_all,
+                0.0,
+            ),
+            axis=2,
         )
         out_pieces = (
             part_out.reshape(heads_local, rows, pieces, sub_width)

time: 610 us -> 529 us (0.87); the launches traced: 598 us -> 525 us
  local copies, waits for them, and re-layouts: 104 us -> 65.3 us
  matrix products: 63.5 us -> 34.8 us
  other arithmetic: 62 us -> 54.4 us
    dot_general x16 -> x4, matrix products: 52.5 us -> 27 us  [the longest x2 14.5 us: per_device(): jnp.einsum('hrc,sc->hrs', q_block, k_cache[layer_index], preferred_elemen...]
    another operation x8 -> x3, local copies, waits for them, and re-layouts: 25.5 us -> 0.02 us  [the longest x2 12.4 us: per_device(): k_cache[layer_index].reshape(step_count, SPAN, heads_local, HEAD_DIM)]
    unnamed x39 -> x44, local copies, waits for them, and re-layouts: 23.7 us -> 0.1 us
    reduce_sum x8 -> x2, other arithmetic: 26.7 us -> 9.83 us  [per_device(): part_sum = jnp.sum(weights, axis=2)]
    dot_general x0 -> x3, local copies, waits for them, and re-layouts: none -> 12.4 us  [per_device(): jnp.einsum('hrs,sc->hrc', weights.astype(jnp.bfloat16), v_cache[layer_ind...]
    slice x2 -> x0, local copies, waits for them, and re-layouts: 9.16 us -> none  [the longest x1 4.63 us: per_device(): v_cache[layer_index].reshape(step_count, SPAN, heads_local, HEAD_DIM)]
where the time goes in v3:
time: 529 us; the launch traced here: 525 us
  Pallas kernels  369 us (70%)
  local copies, waits for them, and re-layouts  65.3 us (12%)
  other arithmetic  54.4 us (10%)
  matrix products  34.8 us (7%)
    pallas_call x3, Pallas kernels, allreduce(): pl.pallas_call(functools.partial(_allreduce_kernel, n, whole, tp_count),...  239 us
    pallas_call x5, Pallas kernels, all_to_all(): pl.pallas_call(functools.partial(_all_to_all_kernel, n, whole, tp_count),...  130 us
    dot_general x2, matrix products, per_device(): jnp.einsum('hrc,sc->hrs', q_block, k_cache[layer_index], preferred_elemen...  14.5 us
    concatenate x2, local copies, waits for them, and re-layouts, per_device(): message = jnp.concatenate([qkv_part, fc1_part], axis=-1)  13.5 us
    dot_general x2, matrix products, per_device(): jnp.einsum('hrs,sc->hrc', weights.astype(jnp.bfloat16), v_cache[layer_ind...  12.5 us
    dot_general x3, local copies, waits for them, and re-layouts, per_device(): jnp.einsum('hrs,sc->hrc', weights.astype(jnp.bfloat16), v_cache[layer_ind...  12.4 us

profile of v3, /device:TPU:25, one launch (start us, length us, event | category | flops | bytes accessed | tf_op | source)
XLA Modules:
  0.0 524.6 jit_solution(16640433402833977358)
XLA Ops:
  23.5 57.5 %shard_map.145 = bf16[128,32,128]{2,1,0:T(8,128)(2,1)} custom-call(bf16[128,32,128]{2,1,0:T(8,128)(2,1)} %select_select_fusion.x_ref), custom_call_target="tpu_custom_call" | custom-call | tf_op jit(solution)/shard_map/pallas_call | solution.py:116
  97.6 5.0 copy.246
  102.6 8.5 %reshape.634 = bf16[32,128,192]{2,1,0:T(8,128)(2,1)} reshape(bf16[32,2,64,3,64]{4,3,2,1,0:T(4,128)(2,1)} %copy.246) | data formatting | bytes 3145728 | tf_op jit(solution)/shard_map/concatenate | solution.py:244
  111.1 3.5 pad_maximum_fusion.x_ref
  114.7 49.5 %shard_map.146 = bf16[32,128,256]{2,1,0:T(8,128)(2,1)} custom-call(bf16[32,128,256]{2,1,0:T(8,128)(2,1)} %pad_maximum_fusion.x_ref), custom_call_target="tpu_custom_call" | custom-call | tf_op jit(solution)/shard_map/pallas_call | solution.py:156
  164.1 2.8 fusion.150
  170.4 19.4 %shard_map.147 = bf16[32,16,256]{2,1,0:T(8,128)(2,1)} custom-call(bf16[32,16,256]{2,1,0:T(8,128)(2,1)} %broadcast_in_dim.308.x_ref), custom_call_target="tpu_custom_call" | custom-call | tf_op jit(solution)/shard_map/pallas_call | solution.py:156
  190.9 4.5 slice_bitcast_fusion
  195.4 4.0 copy.234
  199.4 4.0 copy.219
  203.4 7.2 %fusion = (f32[8,256]{1,0:T(8,128)S(1)}, f32[8,256,2048]{2,1,0:T(8,128)S(1)}) fusion(pred[256,2048]{1,0:T(8,128)(4,1)S(1)} %copy-done.3, bf16[2,2048,512]{2,1,0:T(8,128)(2,1)} %param.21, pred[8,512]{1,0:T(8,128)(4,1)S(1)} %copy-done.16, bf16[256,512]{1,0:T(8,128)(2,1)S(1)} %copy.218), kind=kOutput, calls=%fused_computation.6 | convolution fusion | flops 4308596736 | bytes 19673088 | tf_op jit(solution)/shard_map/hrc,sc->hrs/dot_general | solution.py:283
  210.6 6.3 %select_reduce_fusion.1 = f32[8,256,64]{1,2,0:T(8,128)S(1)} fusion(pred[8,8]{1,0:T(8,128)(4,1)S(1)} %copy-done.21, bf16[8,64,2048,1]{2,1,0,3:T(8,128)(2,1)S(1)} %bitcast.196, f32[8,256,2048]{2,1,0:T(8,128)S(1)} %get-tuple-element.44, f32[8,256]{1,0:T(8,128)S(1)} %get-tuple-element.43, pred[256,2048]{1,0:T(8,128)(4,1)S(1)} %copy-done.3), kind=kOutput, calls=%fused_computation.19 | convolution fusion | flops 4317904896 | bytes 19931200 | tf_op jit(solution)/shard_map/hrs,sc->hrc/dot_general | solution.py:292
  216.9 4.9 fusion.2
  223.0 23.5 %shard_map.148 = f32[32,24,256]{2,1,0:T(8,128)} custom-call(f32[32,24,256]{2,1,0:T(8,128)} %maximum_maximum_fusion.x_ref), custom_call_target="tpu_custom_call" | custom-call | tf_op jit(solution)/shard_map/pallas_call | solution.py:156
  253.8 90.8 %shard_map.149 = f32[128,32,128]{2,1,0:T(8,128)} custom-call(f32[128,32,128]{2,1,0:T(8,128)} %reshape.603.x_ref), custom_call_target="tpu_custom_call" | custom-call | tf_op jit(solution)/shard_map/pallas_call | solution.py:116
  350.5 4.1 add_convert_fusion
  360.7 14.4 %shard_map.150 = bf16[32,16,256]{2,1,0:T(8,128)(2,1)} custom-call(bf16[32,16,256]{2,1,0:T(8,128)(2,1)} %broadcast_in_dim.322.x_ref), custom_call_target="tpu_custom_call" | custom-call | tf_op jit(solution)/shard_map/pallas_call | solution.py:156
  376.2 7.2 %fusion.1 = (f32[8,256]{1,0:T(8,128)S(1)}, f32[8,256,2048]{2,1,0:T(8,128)S(1)}) fusion(pred[256,2048]{1,0:T(8,128)(4,1)S(1)} %copy-done.3, bf16[2,2048,512]{2,1,0:T(8,128)(2,1)} %param.21, pred[8,512]{1,0:T(8,128)(4,1)S(1)} %copy-done.16, bf16[256,512]{1,0:T(8,128)(2,1)S(1)} %copy.233), kind=kOutput, calls=%fused_computation.7 | convolution fusion | flops 4308596736 | bytes 19673088 | tf_op jit(solution)/shard_map/hrc,sc->hrs/dot_general | solution.py:283
  383.5 6.3 %select_reduce_fusion = f32[8,256,64]{1,2,0:T(8,128)S(1)} fusion(pred[8,8]{1,0:T(8,128)(4,1)S(1)} %copy-done.21, bf16[8,64,2048,1]{2,1,0,3:T(8,128)(2,1)S(1)} %bitcast.195, f32[8,256,2048]{2,1,0:T(8,128)S(1)} %get-tuple-element.46, f32[8,256]{1,0:T(8,128)S(1)} %get-tuple-element.45, pred[256,2048]{1,0:T(8,128)(4,1)S(1)} %copy-done.3), kind=kOutput, calls=%fused_computation.18 | convolution fusion | flops 4317904896 | bytes 19931200 | tf_op jit(solution)/shard_map/hrs,sc->hrc/dot_general | solution.py:292
  389.7 4.9 fusion.4
  395.8 23.4 %shard_map.151 = f32[32,24,256]{2,1,0:T(8,128)} custom-call(f32[32,24,256]{2,1,0:T(8,128)} %maximum_maximum_fusion.1.x_ref), custom_call_target="tpu_custom_call" | custom-call | tf_op jit(solution)/shard_map/pallas_call | solution.py:156
  426.6 90.6 %shard_map.152 = f32[128,32,128]{2,1,0:T(8,128)} custom-call(f32[128,32,128]{2,1,0:T(8,128)} %reshape.611.x_ref), custom_call_target="tpu_custom_call" | custom-call | tf_op jit(solution)/shard_map/pallas_call | solution.py:116
  517.3 4.2 fusion.42
  521.5 2.9 add.311
  (218 shorter events, 74.1 us)
Async XLA Ops:
  0.0 19.1 %copy-start = (bf16[400,2048]{1,0:T(8,128)(2,1)S(1)}, bf16[400,2048]{1,0:T(8,128)(2,1)}, u32[]{:S(2)}) copy-start(bf16[400,2048]{1,0:T(8,128)(2,1)} %param.16) | copy-start | bytes 4915204
  0.0 18.5 %copy-start.9 = (bf16[2,64,3,512]{3,1,2,0:T(8,128)(2,1)S(1)}, bf16[2,64,3,512]{3,1,2,0:T(8,128)(2,1)}, u32[]{:S(2)}) copy-start(bf16[2,64,3,512]{3,1,2,0:T(8,128)(2,1)} %param.25) | copy-start | bytes 1179652
  80.9 2.5 copy-start.2
  85.3 3.6 copy-start.7
  92.6 2.8 copy-start.20
  164.1 2.8 copy-start.4
  167.0 0.8 copy-start.13
  167.0 0.8 copy-start.14
  167.0 1.7 copy-start.15
  199.4 4.0 copy-start.3
  199.4 4.0 copy-start.16
  203.3 7.3 %copy-start.6 = (bf16[512,2048]{1,0:T(8,128)(2,1)S(1)}, bf16[512,2048]{1,0:T(8,128)(2,1)}, u32[]{:S(2)}) copy-start(bf16[512,2048]{1,0:T(8,128)(2,1)} %copy.219) | copy-start | bytes 6291460
  203.3 7.3 %copy-start.21 = (pred[8,8]{1,0:T(8,128)(4,1)S(1)}, pred[8,8]{1,0:T(8,128)(4,1)}, u32[]{:S(2)}) copy-start(pred[8,8]{1,0:T(8,128)(4,1)} %iota_compare_fusion.3) | copy-start | bytes 196
  216.9 5.1 copy-start.17
  221.8 26.9 %copy-start.10 = (bf16[2,16,2048]{2,1,0:T(8,128)(2,1)S(1)}, bf16[2,16,2048]{2,1,0:T(8,128)(2,1)}, u32[]{:S(2)}) copy-start(bf16[2,16,2048]{2,1,0:T(8,128)(2,1)} %param.28) | copy-start | bytes 393220
  223.0 26.3 %copy-start.8 = (bf16[2,64,2048]{2,1,0:T(8,128)(2,1)S(1)}, bf16[2,64,2048]{2,1,0:T(8,128)(2,1)}, u32[]{:S(2)}) copy-start(bf16[2,64,2048]{2,1,0:T(8,128)(2,1)} %param.29) | copy-start | bytes 1572868
  223.0 26.3 %copy-start.19 = (f32[64]{0:T(128)S(1)}, f32[64]{0:T(128)}, u32[]{:S(2)}) copy-start(f32[64]{0:T(128)} %get-tuple-element.47) | copy-start | bytes 772
  346.9 3.5 copy-start.12
  376.2 7.3 %copy-start.5 = (bf16[512,2048]{1,0:T(8,128)(2,1)S(1)}, bf16[512,2048]{1,0:T(8,128)(2,1)}, u32[]{:S(2)}) copy-start(bf16[512,2048]{1,0:T(8,128)(2,1)} %copy.234) | copy-start | bytes 6291460
  394.7 26.9 %copy-start.11 = (bf16[2,16,2048]{2,1,0:T(8,128)(2,1)S(1)}, bf16[2,16,2048]{2,1,0:T(8,128)(2,1)}, u32[]{:S(2)}) copy-start(bf16[2,16,2048]{2,1,0:T(8,128)(2,1)} %param.28) | copy-start | bytes 393220
  395.8 26.2 %copy-start.18 = (f32[64]{0:T(128)S(1)}, f32[64]{0:T(128)}, u32[]{:S(2)}) copy-start(f32[64]{0:T(128)} %get-tuple-element.48) | copy-start | bytes 772
  517.3 7.1 %copy-start.1 = (bf16[400,2048]{1,0:T(8,128)(2,1)S(1)}, bf16[400,2048]{1,0:T(8,128)(2,1)}, u32[]{:S(2)}) copy-start(bf16[400,2048]{1,0:T(8,128)(2,1)} %param.16) | copy-start | bytes 4915204
